TPU v7x, 32 devices: a whole 2x2x4 slice. The times are simulated.
32 devices in a mesh: src: 8 (over y, x, core), tgt: 4 (over z).
Axes of the slice: x: 2, y: 2, z: 4, core: 2. Of those that a mesh axis runs over, the one named last changes fastest.
Arguments:
- src_points: bfloat16 [64, 4096], P(None, ('src', 'tgt')), may hold values from -3 to 3
- tgt_points: bfloat16 [64, 1024], P(None, 'tgt'), may hold values from -3 to 3
- src_log_mass: float32 [4096], P(('src', 'tgt')), may hold values from -4 to 4
- tgt_log_mass: bfloat16 [1024], P('tgt'), may hold values from -4 to 4
- tgt_potential: bfloat16 [1024], P('tgt'), may hold values from -18 to 168
- src_cluster: int32 [4096], P(('src', 'tgt')), may hold values from 0 to 63, as said below
- tgt_cluster: int32 [1024], P('tgt'), may hold values from 0 to 63, as said below
- kept_pairs: int32 [1024, 2], replicated, may hold values from 0 to 63, as said below
Outputs:
- new_src_potential: float32 [4096], P(('src', 'tgt'))
- new_tgt_potential: float32 [1024], P('tgt')
Inputs may be any that keep to these rules, and one draw needn't show every extreme that they name: `src_cluster`: never falls along the cells; every cluster holds at least one cell. `tgt_cluster`: never falls along the cells; every cluster holds at least one cell. `kept_pairs`: each pair stands once; every cluster of either day is in some pair.
All inputs are finite; a program needn't handle non-finite values.
Results may differ from a plain program's by a relative error of at most 0.00045.
Values may be sent and summed in bfloat16 or wider, within the bound.
No kernel may reach another device: no remote copies, remote signals or barrier semaphores. Data moves between devices by JAX's collectives and lax.ppermute only.
A program may use at most 128 MiB of HBM per device.

v0:
```python
import math
import jax
import jax.numpy as jnp
from jax import lax
from jax.sharding import PartitionSpec as P

DIM = 64
CLUSTERS = 64
FLOOR_VALUE = -1e30
EPSILON = 1.0
MASS_FACTOR = 10.0 / 11.0
TILE_WIDTH = 2048


def square_norms(points):
    widened = points.astype(jnp.float32)
    return jnp.sum(widened * widened, axis=0)


def cross_products(left_rows, right_rows):
    return lax.dot_general(
        left_rows, right_rows, (((0,), (0,)), ((), ())), preferred_element_type=jnp.float32
    )


def build_grid(kept_pairs, labels):
    src_side = (kept_pairs[:, 0][:, None] == labels[None, :]).astype(jnp.float32)
    tgt_side = (kept_pairs[:, 1][:, None] == labels[None, :]).astype(jnp.float32)
    return jnp.dot(src_side.T, tgt_side, preferred_element_type=jnp.float32)


def body(
    src_points,
    tgt_points,
    src_log_mass,
    tgt_log_mass,
    tgt_potential,
    src_cluster,
    tgt_cluster,
    kept_pairs,
):
    labels = jnp.arange(CLUSTERS, dtype=jnp.int32)
    pair_grid = build_grid(kept_pairs, labels)
    src_norms = square_norms(src_points)
    src_onehot = (src_cluster[:, None] == labels[None, :]).astype(jnp.float32)
    row_grid = jnp.dot(src_onehot, pair_grid, preferred_element_type=jnp.float32)
    reach = jnp.max(row_grid, axis=0)
    row_table = row_grid.astype(jnp.bfloat16)
    row_count = src_points.shape[1]
    block_width = tgt_points.shape[1]
    side_terms = jnp.stack([tgt_potential, tgt_log_mass, tgt_cluster.astype(jnp.bfloat16)], axis=0)
    packed = jnp.concatenate([tgt_points, side_terms], axis=0)

    def unpack(tile):
        tile_points = tile[:DIM]
        tile_labels = tile[DIM + 2].astype(jnp.int32)
        tgt_onehot = labels[:, None] == tile_labels[None, :]
        has_work = jnp.sum(reach * jnp.max(tgt_onehot.astype(jnp.float32), axis=1)) > 0.5
        return (tile_points, tgt_onehot.astype(jnp.bfloat16), has_work)

    def row_tile(running, tile):
        tile_points, tgt_onehot, has_work = unpack(tile)

        def row_compute(current):
            peak_row, sum_row = current
            kept_mask = jnp.dot(row_table, tgt_onehot, preferred_element_type=jnp.float32) > 0.5
            tile_bias = (
                tile[DIM].astype(jnp.float32) - square_norms(tile_points)
            ) / EPSILON + tile[DIM + 1].astype(jnp.float32)
            scores = (
                tile_bias[None, :]
                - (src_norms[:, None] - 2.0 * cross_products(src_points, tile_points)) / EPSILON
            )
            scores = jnp.where(kept_mask, scores, FLOOR_VALUE)
            new_peak = jnp.maximum(peak_row, jnp.max(scores, axis=1))
            weights = jnp.where(kept_mask, jnp.exp(scores - new_peak[:, None]), 0.0)
            return (new_peak, sum_row * jnp.exp(peak_row - new_peak) + jnp.sum(weights, axis=1))

        return lax.cond(has_work, row_compute, lambda current: current, running)

    start_state = (
        jnp.full((row_count,), FLOOR_VALUE, jnp.float32),
        jnp.zeros((row_count,), jnp.float32),
    )
    targets = lax.all_gather(packed, "tgt", axis=1, tiled=True)
    columns = targets.shape[1]
    tile_width = math.gcd(columns, TILE_WIDTH)

    def advance(number, current):
        return row_tile(
            current, lax.dynamic_slice_in_dim(targets, number * tile_width, tile_width, 1)
        )

    peak_row, sum_row = lax.fori_loop(0, columns // tile_width, advance, start_state)
    new_src = -MASS_FACTOR * EPSILON * (peak_row + jnp.log(sum_row))
    col_bias = (new_src - src_norms) / EPSILON + src_log_mass
    column_targets = lax.all_gather(packed, "tgt", axis=1, tiled=True)
    columns = column_targets.shape[1]
    column_tile_width = math.gcd(columns, TILE_WIDTH)

    def column_tile(number):
        tile = lax.dynamic_slice_in_dim(
            column_targets, number * column_tile_width, column_tile_width, 1
        )
        tile_points, tgt_onehot, has_work = unpack(tile)

        def column_compute(unused):
            kept_mask = jnp.dot(row_table, tgt_onehot, preferred_element_type=jnp.float32) > 0.5
            scores = (
                col_bias[:, None]
                - (
                    square_norms(tile_points)[None, :]
                    - 2.0 * cross_products(src_points, tile_points)
                )
                / EPSILON
            )
            scores = jnp.where(kept_mask, scores, FLOOR_VALUE)
            highest = jnp.max(scores, axis=0)
            weights = jnp.where(kept_mask, jnp.exp(scores - highest[None, :]), 0.0)
            return (highest, jnp.sum(weights, axis=0))

        def skipped(unused):
            return (
                jnp.full((column_tile_width,), FLOOR_VALUE, jnp.float32),
                jnp.zeros((column_tile_width,), jnp.float32),
            )

        return lax.cond(has_work, column_compute, skipped, 0)

    peaks, totals = lax.map(column_tile, jnp.arange(columns // column_tile_width, dtype=jnp.int32))
    piece_peak = peaks.reshape(columns)
    piece_sum = totals.reshape(columns)
    stacked = jnp.stack([piece_peak, piece_sum], axis=0)
    col_peak, col_sum = (stacked[0], stacked[1])
    block_offset = lax.axis_index("tgt") * block_width
    global_peak = lax.pmax(col_peak, ("src", "tgt"))
    rescaled = col_sum * jnp.exp(col_peak - global_peak)
    own_share = lax.psum_scatter(rescaled, "tgt", scatter_dimension=0, tiled=True)
    own_sum = lax.psum(own_share, "src")
    own_peak = lax.dynamic_slice_in_dim(global_peak, block_offset, block_width, 0)
    new_tgt = -MASS_FACTOR * EPSILON * (own_peak + jnp.log(own_sum))
    return (new_src, new_tgt)


def solution(mesh):
    in_specs = (
        P(None, ("src", "tgt")),
        P(None, "tgt"),
        P(("src", "tgt")),
        P("tgt"),
        P("tgt"),
        P(("src", "tgt")),
        P("tgt"),
        P(),
    )
    out_specs = (P(("src", "tgt")), P("tgt"))
    return jax.shard_map(body, mesh=mesh, in_specs=in_specs, out_specs=out_specs, check_vma=False)
```

profile of v0, /device:TPU:0, one launch (start us, length us, event | category | flops | bytes accessed | tf_op | source)
XLA Modules:
  0.0 92.5 jit_solution(2774065129864218746)
XLA Ops:
  0.6 0.7 convert_element_type.50
  1.3 0.6 copy-done.4
  2.0 0.6 copy-done.5
  2.6 0.8 pad_maximum_fusion
  3.4 15.2 %all_gather.4 = bf16[67,1024]{1,0:T(8,128)(2,1)S(1)} all-gather(bf16[67,256]{1,0:T(8,128)(2,1)S(1)} %pad_maximum_fusion), channel_id=1, replica_groups=mesh['src'=8,'tgt'=4] {'tgt'}, dimensions={1}, use_global_device_ids=true | all-gather | bytes 171520 | tf_op jit(solution)/shard_map/all_gather | solution.py:85
  18.6 0.0 copy-start.1
  18.6 0.7 copy-done.1
  19.3 0.6 copy-done.6
  20.0 0.9 fusion.18
  20.8 0.0 copy-start
  20.9 0.7 copy-done
  21.6 0.1 convert_reduce_fusion
  21.7 0.6 multiply_reduce_fusion.3
  23.0 1.0 %conditional.2 = ((f32[128]{0:T(128)S(1)}, f32[128]{0:T(128)S(1)})) conditional(s32[]{:T(128)} %convert_element_type.52, (f32[128]{0:T(128)S(1)}, f32[128]{0:T(128)S(1)}) %tuple.37, (bf16[128,64]{0,1:T(8,128)(2,1)S(1)}, bf16[64,1024]{1,0:T(8,128)(2,1)S(1)}, bf16[67,1024]{1,0:T(8,128)(2,1)S(1)}, bf16[64,1024]{1,0:T(8,128)(2,1)S(1)}, f32[128]{0:T(128)S(1)}, ...), branch_computations={%region_4.5_spmd, %region_5.9_spmd} | conditional | flops 34934016 | bytes 1895448 | solution.py:79
  23.0 0.3 convolution_compare_fusion
  23.3 0.4 fusion.16
  23.7 0.3 select_reduce_fusion
  24.0 0.0 copy-start.3
  24.0 0.0 copy-start.2
  24.0 0.6 copy-done.2
  24.7 2.0 %conditional.3 = (f32[1024]{0:T(1024)}, f32[1024]{0:T(1024)S(1)}) conditional(s32[]{:T(128)} %convert_element_type.52, () %tuple.39, (bf16[128,64]{0,1:T(8,128)(2,1)S(1)}, bf16[64,1024]{1,0:T(8,128)(2,1)S(1)}, f32[128]{0:T(128)S(1)}, f32[128]{0:T(128)S(1)}, f32[128]{0:T(128)S(1)}, /*index=5*/bf16[64,1024]{1,0:T(8,128)(2,1)S(1)}, ...), branch_computations={%region_9.10_spmd, %region_10.14_spmd} | conditional | flops 34927872 | bytes 1890832 | solution.py:128
  24.7 0.2 convolution_compare_fusion.1
  25.0 0.9 fusion.17
  25.9 0.8 select_reduce_fusion.1
  26.7 40.9 %pmax.7 = f32[1024]{0:T(1024)S(1)} all-reduce(f32[1024]{0:T(1024)} %get-tuple-element.126), channel_id=1, replica_groups=mesh['src'=8,'tgt'=4] {'src','tgt'}, use_global_device_ids=true, to_apply=%region_14.15 | all-reduce | flops 1024 | bytes 8192 | tf_op jit(solution)/shard_map/pmax | solution.py:136
  67.6 0.7 exponential_multiply_fusion
  68.3 9.8 %all-reduce = f32[1024]{0:T(1024)S(1)} all-reduce(f32[1024]{0:T(1024)S(1)} %exponential_multiply_fusion), channel_id=2, replica_groups=mesh['src'=8,'tgt'=4] {'tgt'}, use_global_device_ids=true, to_apply=%region_15.16.clone | all-reduce | flops 1024 | bytes 8192
  78.1 0.7 copy-done.7
  78.8 0.6 dynamic-slice
  80.0 0.1 dynamic-slice.1
  80.1 11.8 %psum.7 = f32[256]{0:T(256)S(1)} all-reduce(f32[256]{0:T(256)S(1)} %dynamic-slice.1), channel_id=1, replica_groups=mesh['src'=8,'tgt'=4] {'src'}, use_global_device_ids=true, to_apply=%region_16.0 | all-reduce | flops 256 | bytes 2048 | tf_op jit(solution)/shard_map/psum | solution.py:139
  91.9 0.6 add_multiply_fusion
  (23 shorter events, 0.2 us)
Async XLA Ops:
  1.3 0.7 copy-start.4
  2.0 0.7 copy-start.5
  18.6 0.7 copy-start.1
  19.3 0.7 copy-start.6
  20.8 0.7 copy-start
  24.0 0.7 copy-start.3
  24.0 0.7 copy-start.2
  78.1 0.7 copy-start.7
where the time goes:
time: 93.2 us; the launch traced here: 92.5 us
  blocking collectives  77.7 us (83%)
  local copies, waits for them, and re-layouts  5.31 us (6%)
  other arithmetic  4.79 us (5%)
  matrix products  2.63 us (3%)
  between operations  2.03 us (2%)
    pmax x1, blocking collectives, body(): global_peak = lax.pmax(col_peak, ('src', 'tgt'))  40.9 us
    all_gather x1, blocking collectives, body(): targets = lax.all_gather(packed, 'tgt', axis=1, tiled=True)  15.2 us
    psum x1, blocking collectives, body(): own_sum = lax.psum(own_share, 'src')  11.8 us
    unnamed x1, blocking collectives  9.85 us
    unnamed x18, local copies, waits for them, and re-layouts  5.27 us

commit v1 on v0

--- a/solution.py
+++ b/solution.py
@@ -136,7 +136,9 @@
     global_peak = lax.pmax(col_peak, ("src", "tgt"))
     rescaled = col_sum * jnp.exp(col_peak - global_peak)
     own_share = lax.psum_scatter(rescaled, "tgt", scatter_dimension=0, tiled=True)
-    own_sum = lax.psum(own_share, "src")
+    own_sum = own_share
+    for hop in (1, 2, 4):
+        own_sum = own_sum + lax.ppermute(own_sum, "src", [(dev, dev ^ hop) for dev in range(8)])
     own_peak = lax.dynamic_slice_in_dim(global_peak, block_offset, block_width, 0)
     new_tgt = -MASS_FACTOR * EPSILON * (own_peak + jnp.log(own_sum))
     return (new_src, new_tgt)

time: 93.2 us -> 89.8 us (0.964)
  blocking collectives: 77.7 us -> 65.9 us
  starting transfers between devices: 0 us -> 4.3 us
  waiting for transfers between devices: 0 us -> 4.26 us
    psum x1 -> x0, blocking collectives: 11.8 us -> none  [body(): own_sum = lax.psum(own_share, 'src')]
    ppermute x0 -> x3, starting transfers between devices: none -> 4.3 us  [body(): lax.ppermute(own_sum, 'src', [(dev, dev ^ hop) for dev in range(8)])]
    ppermute x0 -> x3, waiting for transfers between devices: none -> 4.26 us  [body(): lax.ppermute(own_sum, 'src', [(dev, dev ^ hop) for dev in range(8)])]
  transfers between devices with their start and end apart: 0 -> 3, of which waited for: 0 -> 3; matrix products, arithmetic and copies ran while one was open for 0% -> 0% of each run, Pallas kernels for 0% -> 0%
where the time goes in v1:
time: 89.8 us; the launch traced here: 89.1 us
  blocking collectives  65.9 us (73%)
  local copies, waits for them, and re-layouts  5.03 us (6%)
  other arithmetic  4.87 us (5%)
  starting transfers between devices  4.3 us (5%)
  waiting for transfers between devices  4.26 us (5%)
  matrix products  2.64 us (3%)
  between operations  2.04 us (2%)
    pmax x1, blocking collectives, body(): global_peak = lax.pmax(col_peak, ('src', 'tgt'))  40.8 us
    all_gather x1, blocking collectives, body(): targets = lax.all_gather(packed, 'tgt', axis=1, tiled=True)  15.2 us
    unnamed x1, blocking collectives  9.94 us
    unnamed x18, local copies, waits for them, and re-layouts  4.99 us
    ppermute x3, starting transfers between devices, body(): lax.ppermute(own_sum, 'src', [(dev, dev ^ hop) for dev in range(8)])  4.3 us
    ppermute x3, waiting for transfers between devices, body(): lax.ppermute(own_sum, 'src', [(dev, dev ^ hop) for dev in range(8)])  4.26 us
  transfers between devices with their start and end apart: 3, of which 3 were waited for; matrix products, arithmetic and copies ran while one was open for 0% of the time, Pallas kernels for 0%

profile of v1, /device:TPU:0, one launch (start us, length us, event | category | flops | bytes accessed | tf_op | source)
XLA Modules:
  0.0 89.1 jit_solution(17619792293555911483)
XLA Ops:
  0.6 0.7 convert_element_type.50
  1.3 0.6 copy-done.4
  2.0 0.6 copy-done.5
  2.6 0.8 pad_maximum_fusion
  3.4 15.2 %all_gather.4 = bf16[67,1024]{1,0:T(8,128)(2,1)S(1)} all-gather(bf16[67,256]{1,0:T(8,128)(2,1)S(1)} %pad_maximum_fusion), channel_id=1, replica_groups=mesh['src'=8,'tgt'=4] {'tgt'}, dimensions={1}, use_global_device_ids=true | all-gather | bytes 171520 | tf_op jit(solution)/shard_map/all_gather | solution.py:85
  18.7 0.1 convert_reduce_fusion
  18.8 0.5 copy-done.1
  19.4 0.7 copy-done.6
  20.1 0.9 fusion.18
  20.9 0.6 multiply_reduce_fusion.3
  22.2 1.0 %conditional.2 = ((f32[128]{0:T(128)S(1)}, f32[128]{0:T(128)S(1)})) conditional(s32[]{:T(128)} %convert_element_type.52, (f32[128]{0:T(128)S(1)}, f32[128]{0:T(128)S(1)}) %tuple.37, (bf16[128,64]{0,1:T(8,128)(2,1)S(1)}, bf16[64,1024]{1,0:T(8,128)(2,1)S(1)}, bf16[67,1024]{1,0:T(8,128)(2,1)S(1)}, bf16[64,1024]{1,0:T(8,128)(2,1)S(1)}, f32[128]{0:T(128)S(1)}, ...), branch_computations={%region_4.5_spmd, %region_5.9_spmd} | conditional | flops 34934016 | bytes 1895448 | solution.py:79
  22.2 0.2 convolution_compare_fusion
  22.6 0.4 fusion.16
  22.9 0.3 select_reduce_fusion
  23.3 0.6 copy-done.2
  23.9 0.5 copy-done.3
  24.4 2.0 %conditional.3 = (f32[1024]{0:T(1024)}, f32[1024]{0:T(1024)S(1)}) conditional(s32[]{:T(128)} %convert_element_type.52, () %tuple.39, (bf16[128,64]{0,1:T(8,128)(2,1)S(1)}, bf16[64,1024]{1,0:T(8,128)(2,1)S(1)}, f32[128]{0:T(128)S(1)}, f32[128]{0:T(128)S(1)}, f32[128]{0:T(128)S(1)}, /*index=5*/bf16[64,1024]{1,0:T(8,128)(2,1)S(1)}, ...), branch_computations={%region_9.10_spmd, %region_10.14_spmd} | conditional | flops 34927872 | bytes 1890832 | solution.py:128
  24.4 0.3 convolution_compare_fusion.1
  24.7 0.9 %fusion.17 = (f32[1024]{0:T(1024)}, f32[128,1024]{1,0:T(8,128)S(1)}) fusion(pred[128,1024]{1,0:T(32,128)(4,1)S(1)} %convolution_compare_fusion.1, bf16[64,128]{1,0:T(8,128)(2,1)S(1)} %get-tuple-element.117, bf16[64,1024]{1,0:T(8,128)(2,1)S(1)} %get-tuple-element.116, f32[1024]{0:T(1024)S(1)} %multiply_reduce_fusion.1, f32[128]{0:T(128)S(1)} %subtract_add_fusion), kind=kOutput, calls=%fused_computation.37 | convolution fusion | flops 17431552 | bytes 811520 | tf_op jit(solution)/shard_map/while/body/eval_jaxpr/cond/branch_1_fun/dot_general | solution.py:21
  25.6 0.8 select_reduce_fusion.1
  26.5 40.8 %pmax.7 = f32[1024]{0:T(1024)S(1)} all-reduce(f32[1024]{0:T(1024)} %get-tuple-element.126), channel_id=1, replica_groups=mesh['src'=8,'tgt'=4] {'src','tgt'}, use_global_device_ids=true, to_apply=%region_14.15 | all-reduce | flops 1024 | bytes 8192 | tf_op jit(solution)/shard_map/pmax | solution.py:136
  67.3 0.7 exponential_multiply_fusion
  67.9 9.9 %all-reduce = f32[1024]{0:T(1024)S(1)} all-reduce(f32[1024]{0:T(1024)S(1)} %exponential_multiply_fusion), channel_id=2, replica_groups=mesh['src'=8,'tgt'=4] {'tgt'}, use_global_device_ids=true, to_apply=%region_15.16.clone | all-reduce | flops 1024 | bytes 8192
  77.9 0.6 copy-done.7
  78.5 0.6 dynamic-slice
  79.8 0.1 dynamic-slice.1
  79.9 1.1 %collective-permute-done = f32[256]{0:T(256)S(1)} collective-permute-done((f32[256]{0:T(256)S(1)}, f32[256]{0:T(256)S(1)}, u32[]{:S(2)}, u32[]{:S(2)}) %collective-permute-start) | collective-permute-done | bytes 1056 | tf_op jit(solution)/shard_map/ppermute | solution.py:141
  81.1 2.3 %collective-permute-start.1 = (f32[256]{0:T(256)S(1)}, f32[256]{0:T(256)S(1)}, u32[]{:S(2)}, u32[]{:S(2)}) collective-permute-start(f32[256]{0:T(256)S(1)} %dynamic-slice_add_fusion), channel_id=1, source_target_pairs={{0,8},{4,12},{8,0},{12,4},{16,24},{20,28},{24,16},{28,20},{1,9},{5... | collective-permute-start | bytes 3080 | tf_op jit(solution)/shard_map/ppermute | solution.py:141
  83.4 1.6 %collective-permute-done.1 = f32[256]{0:T(256)S(1)} collective-permute-done((f32[256]{0:T(256)S(1)}, f32[256]{0:T(256)S(1)}, u32[]{:S(2)}, u32[]{:S(2)}) %collective-permute-start.1) | collective-permute-done | bytes 1056 | tf_op jit(solution)/shard_map/ppermute | solution.py:141
  84.9 2.0 %collective-permute-start.2 = (f32[256]{0:T(256)S(1)}, f32[256]{0:T(256)S(1)}, u32[]{:S(2)}, u32[]{:S(2)}) collective-permute-start(f32[256]{0:T(256)S(1)} %add.44), channel_id=1, source_target_pairs={{0,16},{4,20},{8,24},{12,28},{16,0},{20,4},{24,8},{28,12},{1,17},{... | collective-permute-start | bytes 3080 | tf_op jit(solution)/shard_map/ppermute | solution.py:141
  86.9 1.6 %collective-permute-done.2 = f32[256]{0:T(256)S(1)} collective-permute-done((f32[256]{0:T(256)S(1)}, f32[256]{0:T(256)S(1)}, u32[]{:S(2)}, u32[]{:S(2)}) %collective-permute-start.2) | collective-permute-done | bytes 1056 | tf_op jit(solution)/shard_map/ppermute | solution.py:141
  88.5 0.6 add_multiply_fusion
  (30 shorter events, 0.4 us)
Async XLA Ops:
  1.3 0.7 copy-start.4
  2.0 0.7 copy-start.5
  18.6 0.7 copy-start.1
  18.7 0.7 copy-start
  19.4 0.7 copy-start.6
  23.2 0.7 copy-start.2
  23.9 0.5 copy-start.3
  77.9 0.7 copy-start.7
  79.8 1.2 %collective-permute-start = (f32[256]{0:T(256)S(1)}, f32[256]{0:T(256)S(1)}, u32[]{:S(2)}, u32[]{:S(2)}) collective-permute-start(f32[256]{0:T(256)S(1)} %dynamic-slice.1), channel_id=1, source_target_pairs={{0,4},{4,0},{8,12},{12,8},{16,20},{20,16},{24,28},{28,24},{1,5},{5... | collective-permute-start | bytes 3080 | tf_op jit(solution)/shard_map/ppermute | solution.py:141
  81.1 3.8 %collective-permute-start.1 = (f32[256]{0:T(256)S(1)}, f32[256]{0:T(256)S(1)}, u32[]{:S(2)}, u32[]{:S(2)}) collective-permute-start(f32[256]{0:T(256)S(1)} %dynamic-slice_add_fusion), channel_id=1, source_target_pairs={{0,8},{4,12},{8,0},{12,4},{16,24},{20,28},{24,16},{28,20},{1,9},{5... | collective-permute-start | bytes 3080 | tf_op jit(solution)/shard_map/ppermute | solution.py:141
  84.9 3.6 %collective-permute-start.2 = (f32[256]{0:T(256)S(1)}, f32[256]{0:T(256)S(1)}, u32[]{:S(2)}, u32[]{:S(2)}) collective-permute-start(f32[256]{0:T(256)S(1)} %add.44), channel_id=1, source_target_pairs={{0,16},{4,20},{8,24},{12,28},{16,0},{20,4},{24,8},{28,12},{1,17},{... | collective-permute-start | bytes 3080 | tf_op jit(solution)/shard_map/ppermute | solution.py:141
